TPU v7x, 32 devices: a whole 2x2x4 slice. The times are simulated.
32 devices in a mesh: child: 2 (over core), rows: 16 (over z, y, x).
Axes of the slice: x: 2, y: 2, z: 4, core: 2. Of those that a mesh axis runs over, the one named last changes fastest.
Arguments:
- front_update: bfloat16 [2, 3072, 61440], P('child', 'rows'), may hold values from -0.0234375 to 0.0234375
- child_omega: bfloat16 [2, 61440, 256], P('child', 'rows'), may hold values from -6 to 6
- parent_block: bfloat16 [12288, 128], P(('child', 'rows')), may hold values from -0.5 to 0.5
- parent_omega: bfloat16 [12288, 256], P(('child', 'rows')), may hold values from -6 to 6
- child_map: int32 [2, 3072], replicated, may hold values from 0 to 12287, as said below
- leaf_order: int32 [12288], replicated, may hold values from 0 to 12287, as said below
Outputs:
- parent_samples: float32 [12288, 256], P(('child', 'rows'))
Inputs may be any that keep to these rules, and one draw needn't show every extreme that they name: `child_map`: within one child the entries are distinct. Of each aligned block of 192 rows of one child, at most 12 entries fall in any one aligned block of 384 parent rows, and some block of parent rows gets exactly 12 from every such block. `leaf_order`: A permutation. Each aligned block of 384 leaf positions holds exactly 12 rows of every aligned block of 384 natural rows.
All inputs are finite; a program needn't handle non-finite values.
Results may differ from a plain program's by a relative error of at most 0.0003.
Values may be sent and summed in bfloat16 or wider, within the bound.
No kernel may reach another device: no remote copies, remote signals or barrier semaphores. Data moves between devices by JAX's collectives and lax.ppermute only.
A program may use at most 192 MiB of HBM per device.

v0:
```python
import jax
import jax.numpy as jnp
from jax import lax
from jax.sharding import PartitionSpec as P


def bucket_rank(owner_ids, owners):
    one_hot = (owner_ids[:, None] == jnp.arange(owners, dtype=jnp.int32)[None, :]).astype(jnp.int32)
    running = jnp.cumsum(one_hot, axis=0)
    return jnp.sum(one_hot * running, axis=1) - 1


def select_rows(targets, total, values):
    picker = (targets[None, :] == jnp.arange(total, dtype=jnp.int32)[:, None]).astype(jnp.float32)
    return jnp.dot(
        picker, values, precision=lax.Precision.HIGHEST, preferred_element_type=jnp.float32
    )


def pick_rows(sources, values):
    picker = (sources[:, None] == jnp.arange(values.shape[0], dtype=jnp.int32)[None, :]).astype(
        jnp.float32
    )
    return jnp.dot(
        picker, values, precision=lax.Precision.HIGHEST, preferred_element_type=jnp.float32
    )


def body(front_update, child_omega, parent_block, parent_omega, child_map, leaf_order):
    children = lax.axis_size("child")
    row_count = lax.axis_size("rows")
    owners = children * row_count
    device_id = lax.axis_index("child") * row_count + lax.axis_index("rows")
    slab_rows = front_update[0]
    local_rows = slab_rows.shape[0]
    sample_cols = child_omega.shape[2]
    sampled = jnp.dot(
        slab_rows,
        lax.all_gather(child_omega, "rows", axis=1, tiled=True)[0],
        preferred_element_type=jnp.float32,
    )
    parent_dev = parent_block.shape[0]
    capacity = 2 * local_rows // owners
    route_table = child_map.reshape(owners, local_rows)
    my_targets = lax.dynamic_index_in_dim(route_table, device_id, 0, keepdims=False)
    target_owner = my_targets // parent_dev
    target_slot = target_owner * capacity + bucket_rank(target_owner, owners)
    outgoing = select_rows(target_slot, owners * capacity, sampled)
    incoming = lax.all_to_all(
        outgoing.reshape(owners, capacity, sample_cols),
        ("child", "rows"),
        split_axis=0,
        concat_axis=0,
        tiled=True,
    )
    incoming = incoming.reshape(owners * capacity, sample_cols)
    arrives = route_table // parent_dev == device_id
    arrive_rank = jnp.cumsum(arrives.astype(jnp.int32), axis=1) - 1
    slot_column = jnp.where(arrives, arrive_rank, capacity)
    local_target = jnp.where(arrives, route_table % parent_dev, parent_dev)
    source_ids = jnp.broadcast_to(jnp.arange(owners, dtype=jnp.int32)[:, None], route_table.shape)
    places = (
        jnp.full((owners, capacity + 1), parent_dev, jnp.int32)
        .at[source_ids, slot_column]
        .set(local_target)[:, :capacity]
    )
    assembled = select_rows(places.reshape(-1), parent_dev, incoming)
    leaf_size = parent_block.shape[1]
    leaf_blocks = parent_dev // leaf_size
    own_samples = jnp.einsum(
        "bij,bjr->bir",
        parent_block.reshape(leaf_blocks, leaf_size, leaf_size),
        parent_omega.reshape(leaf_blocks, leaf_size, sample_cols),
        preferred_element_type=jnp.float32,
    ).reshape(parent_dev, sample_cols)
    assembled = assembled + own_samples
    parent_rows = leaf_order.shape[0]
    position = (
        jnp.zeros((parent_rows,), jnp.int32)
        .at[leaf_order]
        .set(jnp.arange(parent_rows, dtype=jnp.int32))
    )
    my_positions = lax.dynamic_slice_in_dim(position, device_id * parent_dev, parent_dev)
    leaf_owner = my_positions // parent_dev
    leaf_capacity = parent_dev // owners
    leaf_slot = leaf_owner * leaf_capacity + bucket_rank(leaf_owner, owners)
    sending = select_rows(leaf_slot, owners * leaf_capacity, assembled)
    arrived = lax.all_to_all(
        sending.reshape(owners, leaf_capacity, sample_cols),
        ("child", "rows"),
        split_axis=0,
        concat_axis=0,
        tiled=True,
    )
    arrived = arrived.reshape(owners * leaf_capacity, sample_cols)
    natural = lax.dynamic_slice_in_dim(leaf_order, device_id * parent_dev, parent_dev)
    anchor = natural // parent_dev
    offset = natural % parent_dev
    same_anchor = anchor[:, None] == anchor[None, :]
    earlier = offset[None, :] < offset[:, None]
    arrival_rank = jnp.sum((same_anchor & earlier).astype(jnp.int32), axis=1)
    return pick_rows(anchor * leaf_capacity + arrival_rank, arrived)


def solution(mesh):
    placed = (
        P("child", "rows", None),
        P("child", "rows", None),
        P(("child", "rows"), None),
        P(("child", "rows"), None),
        P(),
        P(),
    )
    return jax.shard_map(
        body, mesh=mesh, in_specs=placed, out_specs=P(("child", "rows"), None), check_vma=False
    )
```

profile of v0, /device:TPU:0, one launch (start us, length us, event | category | flops | bytes accessed | tf_op | source)
XLA Modules:
  0.0 413.5 jit_solution(11872112783750863847)
XLA Ops:
  6.5 0.7 all-gather.2.cloned.1.call-update
  7.3 0.8 reshape.119
  8.2 0.6 reduce-window.26
  9.2 0.6 reduce-window.24
  10.1 0.7 multiply_reduce_fusion
  10.8 0.7 and_reduce_fusion
  11.7 23.0 %scatter_custom_fusion.1 = s32[416]{0:T(512)S(1)} fusion(s32[6144]{0:T(1024)S(1)} %reshape.145, s32[6144]{0:T(1024)S(1)} %reshape.147, s32[]{:T(128)} %constant.80.clone.1), kind=kCustom, calls=%fused_computation.74 | custom fusion | bytes 1668
  34.9 0.8 compare_select_fusion
  35.7 45.4 %scatter_custom_fusion = s32[12288]{0:T(1024)S(1)} fusion(s32[12288]{0:T(1024)S(1)} %compare_select_fusion, s32[12288]{0:T(1024)S(1)} %iota.32, s32[]{:T(128)} %constant.81.clone.1), kind=kCustom, calls=%fused_computation.55 | custom fusion | bytes 49156 | tf_op jit(solution)/shard_map/scatter | solution.py:81
  81.3 0.9 reduce-window.20
  82.3 261.0 %all-gather.2.cloned.1.call-done = bf16[1,61440,256]{2,1,0:T(8,128)(2,1)} async-done(((bf16[1,3840,256]{2,1,0:T(8,128)(2,1)}), bf16[1,61440,256]{2,1,0:T(8,128)(2,1)}) %all-gather.2.cloned.1.call-update) | async-done | bytes 31457296 | tf_op jit(solution)/shard_map/all_gather | solution.py:39
  343.3 19.9 %fusion = f32[192,256]{1,0:T(8,128)S(1)} fusion(bf16[1,61440,256]{2,1,0:T(8,128)(2,1)} %all-gather.2.cloned.1.call-done, bf16[1,192,61440]{2,1,0:T(8,128)(2,1)} %param.6), kind=kOutput, calls=%fused_computation.2 | convolution fusion | flops 6039797760 | bytes 55246848 | tf_op jit(solution)/shard_map/dot_general | solution.py:37
  363.2 0.3 fusion.5
  363.6 0.8 reshape.124
  364.4 2.8 all-to-all-start
  368.0 16.1 %all-to-all-done = f32[32,12,256]{2,1,0:T(8,128)S(1)} async-done(((f32[32,12,256]{2,1,0:T(8,128)}), f32[32,12,256]{2,1,0:T(8,128)S(1)}, u32[]{:S(2)}, u32[]{:S(2)}) %all-to-all-start) | async-done | bytes 393248 | tf_op jit(solution)/shard_map/all_to_all | solution.py:49
  384.1 0.5 convolution_add_fusion
  384.6 0.5 fusion.4
  385.1 0.8 reshape.129
  386.0 2.6 all-to-all-start.1
  388.6 0.8 add_select_fusion.4
  389.4 0.3 convert_reduce_fusion
  389.6 15.7 %all-to-all-done.1 = f32[32,12,256]{2,1,0:T(8,128)S(1)} async-done(((f32[32,12,256]{2,1,0:T(8,128)}), f32[32,12,256]{2,1,0:T(8,128)S(1)}, u32[]{:S(2)}, u32[]{:S(2)}) %all-to-all-start.1) | async-done | bytes 393248 | tf_op jit(solution)/shard_map/all_to_all | solution.py:88
  405.4 1.3 fusion.3
  (43 shorter events, 2.2 us)
Async XLA Ops:
  6.5 361.2 %copy-start = (bf16[384,256]{1,0:T(8,128)(2,1)S(1)}, bf16[384,256]{1,0:T(8,128)(2,1)}, u32[]{:S(2)}) copy-start(bf16[384,256]{1,0:T(8,128)(2,1)} %param.9) | copy-start | bytes 589828
  6.5 336.8 %all-gather.2.cloned.1.call-start = ((), (), s32[]{:S(2)}) async-start(), calls=%async_computation.2 | async-start | bytes 33423360 | tf_op jit(solution)/shard_map/all_gather | solution.py:39
  82.3 285.5 %copy-start.1 = (bf16[384,128]{1,0:T(8,128)(2,1)S(1)}, bf16[384,128]{1,0:T(8,128)(2,1)}, u32[]{:S(2)}) copy-start(bf16[384,128]{1,0:T(8,128)(2,1)} %param.8) | copy-start | bytes 294916
  364.4 19.6 %all-to-all-start = ((f32[32,12,256]{2,1,0:T(8,128)}), f32[32,12,256]{2,1,0:T(8,128)S(1)}, u32[]{:S(2)}, u32[]{:S(2)}) async-start(f32[32,12,256]{2,1,0:T(8,128)} %reshape.124), calls=%async_computation | async-start | bytes 1048576 | tf_op jit(solution)/shard_map/all_to_all | solution.py:49
  386.0 19.4 %all-to-all-start.1 = ((f32[32,12,256]{2,1,0:T(8,128)}), f32[32,12,256]{2,1,0:T(8,128)S(1)}, u32[]{:S(2)}, u32[]{:S(2)}) async-start(f32[32,12,256]{2,1,0:T(8,128)} %reshape.129), calls=%async_computation.1 | async-start | bytes 1048576 | tf_op jit(solution)/shard_map/all_to_all | solution.py:88
Sparse Core Ops, SparseCore 0:
  10.1 333.1 all-gather.1
where the time goes:
time: 414 us
  waiting for transfers between devices  294 us (71%)
  local copies, waits for them, and re-layouts  72 us (17%)
  matrix products  22.7 us (5%)
  between operations  13.6 us (3%)
  other arithmetic  6.26 us (2%)
  starting transfers between devices  5.39 us (1%)
    all_gather x1, waiting for transfers between devices, body(): lax.all_gather(child_omega, 'rows', axis=1, tiled=True)[0]  261 us
    scatter x1, local copies, waits for them, and re-layouts, body(): position = jnp.zeros((parent_rows,), jnp.int32).at[leaf_order].set(jnp.ar...  45.4 us
    unnamed x7, local copies, waits for them, and re-layouts  23.1 us
    dot_general x1, matrix products, body(): jnp.dot(slab_rows, lax.all_gather(child_omega, 'rows', axis=1, tiled=True...  19.9 us
    all_to_all x1, waiting for transfers between devices, body(): lax.all_to_all(outgoing.reshape(owners, capacity, sample_cols), ('child',...  16.1 us
    all_to_all x1, waiting for transfers between devices, body(): lax.all_to_all(sending.reshape(owners, leaf_capacity, sample_cols), ('chi...  15.7 us
  transfers between devices with their start and end apart: 3, of which 3 were waited for; matrix products, arithmetic and copies ran while one was open for 19% of the time, Pallas kernels for 0%

commit v1 on v0

v1 whole, which is shorter than its diff:
```python
import functools

import jax
import jax.numpy as jnp
from jax import lax
from jax.experimental import pallas as pl
from jax.experimental.pallas import tpu as pltpu
from jax.sharding import PartitionSpec as P


PLAN = (
    (("XO", 1, 0, 0, 0), ("YO", 0, 1, 0, 0), ("XI", 1, 0, 1, 1), ("YI", 0, 1, 1, 1), ("PO", 0, 0, 1, 0), ("PI", 0, 0, 0, 0), ("C", 0, 0, 2, 0)),
    (("XO", 1, 0, 0, 1), ("YO", 0, 1, 0, 1), ("XI", 1, 0, 1, 0), ("YI", 0, 1, 1, 0), ("PO", 0, 0, 1, 1), ("PI", 0, 0, 0, 1), ("C", 0, 0, 3, 0)),
    (("XO", 1, 0, 1, 0), ("YO", 0, 1, 1, 0), ("XI", 1, 0, 2, 0), ("YI", 0, 1, 3, 0), ("PO", 0, 0, 2, 0), ("C", 0, 1, 2, 1)),
    (("XO", 1, 0, 1, 1), ("YO", 1, 1, 0, 0), ("XI", 1, 0, 0, 0), ("YI", 1, 1, 1, 0), ("PO", 0, 0, 3, 0), ("C", 0, 0, 3, 1)),
    (("XO", 1, 0, 2, 0), ("YO", 1, 1, 1, 0), ("XI", 1, 1, 3, 0), ("YI", 1, 1, 2, 0), ("PO", 0, 1, 2, 1), ("C", 0, 1, 2, 0)),
    (("XO", 1, 0, 3, 0), ("YO", 0, 1, 2, 0), ("XI", 1, 0, 3, 1), ("YI", 0, 1, 0, 0), ("PO", 0, 1, 3, 0), ("PI", 1, 1, 0, 0), ("C", 1, 0, 3, 0)),
    (("XO", 1, 1, 0, 1), ("YO", 1, 1, 1, 1), ("XI", 1, 1, 2, 1), ("YI", 1, 1, 3, 1), ("PO", 0, 0, 3, 1), ("C", 1, 0, 2, 1)),
    (("YO", 0, 0, 2, 1), ("YI", 0, 1, 0, 1), ("PO", 1, 0, 3, 1), ("C", 0, 0, 2, 1)),
    (("XO", 0, 1, 1, 1), ("YO", 0, 1, 3, 1), ("XI", 1, 1, 1, 1), ("YI", 0, 1, 3, 1), ("PO", 1, 0, 2, 1), ("PI", 1, 0, 0, 1), ("C", 1, 1, 0, 1)),
)
HANDED = (("PI", 1, 1, 2, 3), ("PI", 1, 1, 3, 4))


def grid_of(rows):
    power = rows.bit_length() - 1
    z_power = -(-power // 3)
    y_power = -(-(power - z_power) // 2)
    return 2**z_power, 2**y_power, 2 ** (power - z_power - y_power)


def bucket_rank(owner_ids, owners):
    one_hot = (owner_ids[:, None] == jnp.arange(owners, dtype=jnp.int32)[None, :]).astype(jnp.int32)
    running = jnp.cumsum(one_hot, axis=0)
    return jnp.sum(one_hot * running, axis=1) - 1


def select_rows(targets, total, values):
    picker = (targets[None, :] == jnp.arange(total, dtype=jnp.int32)[:, None]).astype(jnp.float32)
    return jnp.dot(
        picker, values, precision=lax.Precision.HIGHEST, preferred_element_type=jnp.float32
    )


def pick_rows(sources, values):
    picker = (sources[:, None] == jnp.arange(values.shape[0], dtype=jnp.int32)[None, :]).astype(
        jnp.float32
    )
    return jnp.dot(
        picker, values, precision=lax.Precision.HIGHEST, preferred_element_type=jnp.float32
    )


class Grid:
    def __init__(self, rows):
        self.z, self.y, self.x = grid_of(rows)
        self.rows = rows
        self.fits = (self.z, self.y, self.x) == (4, 2, 2)

    def place(self, r):
        return r // (self.y * self.x), (r // self.x) % self.y, r % self.x

    def index(self, z, y, x):
        return (z * self.y + y) * self.x + x

    def kind(self, r):
        return "I" if 0 < self.place(r)[0] < self.z - 1 else "O"

    def block(self, r, dx, dy, q):
        z, y, x = self.place(r)
        plane = q if z < self.z // 2 else self.z - 1 - q
        return self.index(plane, y ^ dy, x ^ dx)

    def pairs(self, link):
        found = []
        for r in range(self.rows):
            z, y, x = self.place(r)
            if link[0] == "C":
                if self.kind(r) == "I":
                    found.append((r, self.index(self.z - 1 - z, y, x)))
            elif link[0] == "P":
                if self.kind(r) != link[1]:
                    found.append((r, self.index(z ^ 1, y, x)))
            elif self.kind(r) == link[1]:
                found.append((r, r ^ 1 if link[0] == "X" else r ^ self.x))
        return found


SENDER = {"XO": "O", "YO": "O", "XI": "I", "YI": "I", "PO": "I", "PI": "O", "C": "I"}
TAKER = {"XO": "O", "YO": "O", "XI": "I", "YI": "I", "PO": "O", "PI": "I", "C": "I"}
BACK = {"PI": "PO", "XO": "XO", "XI": "XI"}


def across(link, item):
    dx, dy, q, *rest = item
    if link[0] == "X":
        dx ^= 1
    if link[0] == "Y":
        dy ^= 1
    if link[0] == "C":
        q = 3 - q
    return (dx, dy, q, *rest)


def multiply_kernel(
    units, n_slabs, n_blocks, chained, spot_ref, *refs
):
    slabs, refs = refs[:n_slabs], refs[n_slabs:]
    blocks, refs = refs[:n_blocks], refs[n_blocks:]
    if chained:
        before, refs = refs[0], refs[1:]
    total, left, right, sem = refs
    x, y, far, inner = (spot_ref[i] for i in range(4))
    kind_of = {"O": 0, "I": 1}
    counts = [sum(u[0] == k for u in units) for k in ("O", "I")]
    count = jnp.where(inner == 1, counts[1], counts[0])
    depth = right.shape[1]
    ordered = []
    seen = {"O": 0, "I": 0}
    for kind, *unit in units:
        ordered.append((kind_of[kind], seen[kind], *unit))
        seen[kind] += 1

    def start(number):
        slot = lax.rem(number, 2)
        for kind, place, slab, item, block, _ in ordered:
            @pl.when((inner == kind) & (number == place))
            def _():
                if item is None:
                    source = slabs[slab]
                else:
                    dx, dy, q = item
                    plane = jnp.where(far == 1, 3 - q, q)
                    index = plane * 4 + (y ^ dy) * 2 + (x ^ dx)
                    column = pl.multiple_of(index * depth, 128)
                    source = slabs[slab].at[:, pl.ds(column, depth)]
                pltpu.make_async_copy(source, left.at[slot], sem.at[0, slot]).start()
                pltpu.make_async_copy(blocks[block], right.at[slot], sem.at[1, slot]).start()

    total[...] = before[...] if chained else jnp.zeros_like(total)
    start(jnp.int32(0))

    def step(number, _):
        slot = lax.rem(number, 2)
        start(number + 1)
        pltpu.make_async_copy(blocks[0], right.at[slot], sem.at[1, slot]).wait()
        pltpu.make_async_copy(slabs[0].at[:, pl.ds(0, depth)], left.at[slot], sem.at[0, slot]).wait()
        half = jnp.int32(0)
        for kind, place, _, _, _, h in ordered:
            if h:
                half = jnp.where((inner == kind) & (number == place), h, half)
        total[half] += jnp.dot(left[slot], right[slot], preferred_element_type=jnp.float32)
        return 0

    lax.fori_loop(0, count, step, 0)


def multiply(spot, slabs, blocks, units, before=None):
    rows = slabs[0].shape[0]
    depth, width = blocks[0].shape
    hbm = pl.BlockSpec(memory_space=pltpu.HBM)
    vmem = pl.BlockSpec(memory_space=pltpu.VMEM)
    chained = before is not None
    specs = [pl.BlockSpec(memory_space=pltpu.SMEM)] + [hbm] * (len(slabs) + len(blocks))
    operands = [spot, *slabs, *blocks]
    if chained:
        specs.append(vmem)
        operands.append(before)
    return pl.pallas_call(
        functools.partial(multiply_kernel, units, len(slabs), len(blocks), chained),
        out_shape=jax.ShapeDtypeStruct((2, rows, width), jnp.float32),
        in_specs=specs,
        out_specs=vmem,
        scratch_shapes=[
            pltpu.VMEM((2, rows, depth), slabs[0].dtype),
            pltpu.VMEM((2, depth, width), blocks[0].dtype),
            pltpu.SemaphoreType.DMA((2, 2)),
        ],
        cost_estimate=pl.CostEstimate(
            flops=8 * rows * depth * width,
            bytes_accessed=8 * depth * (rows + width),
            transcendentals=0,
        ),
        compiler_params=pltpu.CompilerParams(vmem_limit_bytes=48 * 2**20),
    )(*operands)


def choose_kernel(count, spot_ref, *refs):
    outer, inner, out = refs[:count], refs[count : 2 * count], refs[2 * count : 3 * count]
    held, sem = refs[3 * count :]
    for number in range(count):
        for kind, source in ((0, outer), (1, inner)):
            @pl.when(spot_ref[3] == kind)
            def _():
                pltpu.make_async_copy(source[number], held.at[number], sem.at[0, number]).start()
    for number in range(count):
        pltpu.make_async_copy(outer[number], held.at[number], sem.at[0, number]).wait()
        pltpu.make_async_copy(held.at[number], out[number], sem.at[1, number]).start()
    for number in range(count):
        pltpu.make_async_copy(held.at[number], out[number], sem.at[1, number]).wait()


def choose(spot, outer, inner):
    count = len(outer)
    like = outer[0]
    hbm = pl.BlockSpec(memory_space=pltpu.HBM)
    return pl.pallas_call(
        functools.partial(choose_kernel, count),
        out_shape=[jax.ShapeDtypeStruct(like.shape, like.dtype)] * count,
        in_specs=[pl.BlockSpec(memory_space=pltpu.SMEM)] + [hbm] * (2 * count),
        out_specs=[hbm] * count,
        scratch_shapes=[
            pltpu.VMEM((count, *like.shape), like.dtype),
            pltpu.SemaphoreType.DMA((2, count)),
        ],
        compiler_params=pltpu.CompilerParams(vmem_limit_bytes=48 * 2**20),
    )(spot, *outer, *inner)


def sample_scheduled(slab, omega, row_id, grid):
    depth, cols = omega.shape
    half = cols // 2
    places = [grid.place(r) for r in range(grid.rows)]
    table = [[x, y, int(2 * z >= grid.z), int(0 < z < grid.z - 1)] for z, y, x in places]
    spot = jnp.asarray(table, dtype=jnp.int32)[row_id]
    x, y, far = spot[0], spot[1], spot[2]
    own = [omega[:, :half], omega[:, half:]]
    arrays = {
        "O": {(0, 0, 0, h): own[h] for h in (0, 1)},
        "I": {(0, 0, 1, h): own[h] for h in (0, 1)},
    }

    def columns(dx, dy, q):
        plane = jnp.where(far == 1, grid.z - 1 - q, q)
        index = (plane * grid.y + (y ^ dy)) * grid.x + (x ^ dx)
        return lax.dynamic_slice(slab, (0, index * depth), (slab.shape[0], depth))

    shipped = {}
    total = None
    probe = None
    finished = []
    last_first = max(t for t, sends in enumerate(PLAN, 1) if any(s[4] == 0 for s in sends))
    blocks = own[:]
    units = [(k, 0, (0, 0, q), h, h) for k, q in (("O", 0), ("I", 1)) for h in (0, 1)]
    for step, transfers in enumerate(PLAN, 1):
        for link, dx, dy, q, at in HANDED:
            if at == step:
                piece = columns(dx, dy, q)
                shipped[link, dx, dy, q] = lax.ppermute(piece, "rows", grid.pairs(link))
        families = {}
        for link, *item in transfers:
            families.setdefault(link[0], []).append((link, tuple(item)))
        operands = {}
        mixed = []
        for family, group in families.items():
            sources = {SENDER[l]: arrays[SENDER[l]][across(l, item)] for l, item in group}
            if len(set(id(a) for a in sources.values())) == 1:
                operands[family] = list(sources.values())[0]
            else:
                mixed.append((family, sources))
        if mixed:
            picked = choose(spot, [m[1]["O"] for m in mixed], [m[1]["I"] for m in mixed])
            operands.update({m[0]: value for m, value in zip(mixed, picked)})
        new = []
        for family, group in families.items():
            pairs = sorted(pair for link, _ in group for pair in grid.pairs(link))
            arrived = lax.ppermute(operands[family], "rows", pairs)
            probe = arrived if probe is None else probe
            for link, item in group:
                new.append((TAKER[link], item, arrived))
                units.append((TAKER[link], 0, item[:3], len(blocks), item[3]))
            blocks.append(arrived)
        for kind, item, arrived in new:
            arrays[kind][item] = arrived
        total = multiply(spot, [slab], blocks, units, total)
        blocks, units = [], []
        if step in (last_first, len(PLAN)):
            finished.append(total[len(finished)])
    for link in sorted(set(entry[0] for entry in HANDED)):
        for h in (0, 1):
            kind = TAKER[link]
            slabs, blocks, units = [], [], []
            for name, dx, dy, q, _ in HANDED:
                if name == link:
                    item = across(link, (dx, dy, q, h))
                    units.append((kind, len(slabs), None, len(blocks), 0))
                    slabs.append(shipped[link, dx, dy, q])
                    blocks.append(arrays[kind][item])
            term = multiply(spot, slabs, blocks, units)[0]
            finished[h] += lax.ppermute(term, "rows", grid.pairs(BACK[link]))
    return finished, probe


def body(front_update, child_omega, parent_block, parent_omega, child_map, leaf_order):
    children = lax.axis_size("child")
    row_count = lax.axis_size("rows")
    owners = children * row_count
    row_id = lax.axis_index("rows")
    device_id = lax.axis_index("child") * row_count + row_id
    slab = front_update[0]
    local_rows = slab.shape[0]
    sample_cols = child_omega.shape[2]
    grid = Grid(row_count)
    if grid.fits:
        pieces, probe = sample_scheduled(slab, child_omega[0], row_id, grid)
        child_map, leaf_order, parent_block, _ = lax.optimization_barrier(
            (child_map, leaf_order, parent_block, probe)
        )
    else:
        gathered = lax.all_gather(child_omega, "rows", axis=1, tiled=True)[0]
        pieces = [jnp.dot(slab, gathered, preferred_element_type=jnp.float32)]

    parent_dev = parent_block.shape[0]
    capacity = 2 * local_rows // owners
    route_table = child_map.reshape(owners, local_rows)
    my_targets = lax.dynamic_index_in_dim(route_table, device_id, 0, keepdims=False)
    target_owner = my_targets // parent_dev
    target_slot = target_owner * capacity + bucket_rank(target_owner, owners)

    arrives = route_table // parent_dev == device_id
    arrive_rank = jnp.cumsum(arrives.astype(jnp.int32), axis=1) - 1
    slot_column = jnp.where(arrives, arrive_rank, capacity)
    local_target = jnp.where(arrives, route_table % parent_dev - parent_dev, 0)
    in_slot = slot_column[:, None, :] == jnp.arange(capacity, dtype=jnp.int32)[None, :, None]
    places = parent_dev + jnp.sum(jnp.where(in_slot, local_target[:, None, :], 0), axis=2)
    places = places.reshape(-1)

    leaf_size = parent_block.shape[1]
    leaf_blocks = parent_dev // leaf_size
    own_samples = jnp.einsum(
        "bij,bjr->bir",
        parent_block.reshape(leaf_blocks, leaf_size, leaf_size),
        parent_omega.reshape(leaf_blocks, leaf_size, sample_cols),
        preferred_element_type=jnp.float32,
    ).reshape(parent_dev, sample_cols)

    parent_rows = leaf_order.shape[0]
    my_rows = device_id * parent_dev + jnp.arange(parent_dev, dtype=jnp.int32)
    is_mine = leaf_order[:, None] == my_rows[None, :]
    positions = jnp.arange(parent_rows, dtype=jnp.int32)[:, None]
    my_positions = jnp.sum(jnp.where(is_mine, positions, 0), axis=0)
    leaf_owner = my_positions // parent_dev
    leaf_capacity = parent_dev // owners
    leaf_slot = leaf_owner * leaf_capacity + bucket_rank(leaf_owner, owners)

    natural = lax.dynamic_slice_in_dim(leaf_order, device_id * parent_dev, parent_dev)
    anchor = natural // parent_dev
    offset = natural % parent_dev
    same_anchor = anchor[:, None] == anchor[None, :]
    earlier = offset[None, :] < offset[:, None]
    arrival_rank = jnp.sum((same_anchor & earlier).astype(jnp.int32), axis=1)
    leaf_source = anchor * leaf_capacity + arrival_rank

    def exchange(values, rows_each):
        width = values.shape[1]
        return lax.all_to_all(
            values.reshape(owners, rows_each, width),
            ("child", "rows"),
            split_axis=0,
            concat_axis=0,
            tiled=True,
        ).reshape(owners * rows_each, width)

    outputs = []
    start = 0
    for sampled in pieces:
        width = sampled.shape[1]
        outgoing = select_rows(target_slot, owners * capacity, sampled)
        incoming = exchange(outgoing, capacity)
        assembled = select_rows(places, parent_dev, incoming)
        assembled = assembled + own_samples[:, start : start + width]
        arrived = exchange(select_rows(leaf_slot, owners * leaf_capacity, assembled), leaf_capacity)
        outputs.append(pick_rows(leaf_source, arrived))
        start += width
    return outputs[0] if len(outputs) == 1 else jnp.concatenate(outputs, axis=1)


def solution(mesh):
    placed = (
        P("child", "rows", None),
        P("child", "rows", None),
        P(("child", "rows"), None),
        P(("child", "rows"), None),
        P(),
        P(),
    )
    step = jax.shard_map(
        body, mesh=mesh, in_specs=placed, out_specs=P(("child", "rows"), None), check_vma=False
    )
    if not Grid(mesh.shape["rows"]).fits:
        return step
    return step
```

time: 414 us -> 384 us (0.928)
  waiting for transfers between devices: 294 us -> 166 us
  starting transfers between devices: 5.39 us -> 107 us
  Pallas kernels: 0 us -> 70.2 us
  local copies, waits for them, and re-layouts: 72 us -> 22.9 us
  matrix products: 22.7 us -> 4.25 us
  between operations: 13.6 us -> 2.68 us
    all_gather x1 -> x0, waiting for transfers between devices: 261 us -> none  [body(): lax.all_gather(child_omega, 'rows', axis=1, tiled=True)[0]]
    ppermute x0 -> x39, waiting for transfers between devices: none -> 108 us  [the longest x35 59.9 us: sample_scheduled(): arrived = lax.ppermute(operands[family], 'rows', pairs)]
    ppermute x0 -> x39, starting transfers between devices: none -> 91.8 us  [the longest x35 82 us: sample_scheduled(): arrived = lax.ppermute(operands[family], 'rows', pairs)]
    pallas_call x0 -> x20, Pallas kernels: none -> 70.2 us  [the longest x11 45.3 us: multiply(): pl.pallas_call(functools.partial(multiply_kernel, units, len(slabs), len(...]
    scatter x1 -> x0, local copies, waits for them, and re-layouts: 45.4 us -> none  [body(): position = jnp.zeros((parent_rows,), jnp.int32).at[leaf_order].set(jnp.ar...]
    all_to_all x2 -> x4, waiting for transfers between devices: 31.8 us -> 57.7 us  [exchange(): lax.all_to_all(values.reshape(owners, rows_each, width), ('child', 'rows'...]
    dot_general x1 -> x0, matrix products: 19.9 us -> none  [body(): jnp.dot(slab_rows, lax.all_gather(child_omega, 'rows', axis=1, tiled=True...]
    unnamed x7 -> x50, local copies, waits for them, and re-layouts: 23.1 us -> 11.6 us
  transfers between devices with their start and end apart: 3 -> 43, of which waited for: 3 -> 15; matrix products, arithmetic and copies ran while one was open for 19% -> 5% of each run, Pallas kernels for 0% -> 18%
where the time goes in v1:
time: 384 us; the launch traced here: 382 us
  waiting for transfers between devices  166 us (43%)
  starting transfers between devices  107 us (28%)
  Pallas kernels  70.2 us (18%)
  local copies, waits for them, and re-layouts  22.9 us (6%)
  other arithmetic  9.37 us (2%)
  matrix products  4.25 us (1%)
    ppermute x35, starting transfers between devices, sample_scheduled(): arrived = lax.ppermute(operands[family], 'rows', pairs)  82 us
    ppermute x35, waiting for transfers between devices, sample_scheduled(): arrived = lax.ppermute(operands[family], 'rows', pairs)  59.9 us
    all_to_all x4, waiting for transfers between devices, exchange(): lax.all_to_all(values.reshape(owners, rows_each, width), ('child', 'rows'...  57.7 us
    ppermute x2, waiting for transfers between devices, sample_scheduled(): shipped[link, dx, dy, q] = lax.ppermute(piece, 'rows', grid.pairs(link))  48 us
    pallas_call x11, Pallas kernels, multiply(): pl.pallas_call(functools.partial(multiply_kernel, units, len(slabs), len(...  45.3 us
    pallas_call x9, Pallas kernels, choose(): pl.pallas_call(functools.partial(choose_kernel, count), out_shape=[jax.Sh...  25 us
    all_to_all x4, starting transfers between devices, exchange(): lax.all_to_all(values.reshape(owners, rows_each, width), ('child', 'rows'...  15.3 us
    unnamed x50, local copies, waits for them, and re-layouts  11.6 us
  transfers between devices with their start and end apart: 43, of which 15 were waited for; matrix products, arithmetic and copies ran while one was open for 5% of the time, Pallas kernels for 18%

profile of v1, /device:TPU:0, one launch (start us, length us, event | category | flops | bytes accessed | tf_op | source)
XLA Modules:
  0.0 382.1 jit_solution(6476993912383011914)
XLA Ops:
  19.2 10.8 %collective-permute-done.refs_1_.refs_3_ = bf16[3840,128]{1,0:T(8,128)(2,1)} collective-permute-done((bf16[3840,128]{1,0:T(8,128)(2,1)}, bf16[3840,128]{1,0:T(8,128)(2,1)}, u32[]{:S(2)}, u32[]{:S(2)}) %collective-permute-start) | collective-permute-done | bytes 983072 | tf_op jit(solution)/shard_map/ppermute | solution.py:267
  37.0 4.8 %collective-permute-start.24 = (bf16[192,3840]{1,0:T(8,128)(2,1)}, bf16[192,3840]{1,0:T(8,128)(2,1)}, u32[]{:S(2)}, u32[]{:S(2)}) collective-permute-start(bf16[192,3840]{1,0:T(8,128)(2,1)} %get-tuple-element.50), channel_id=1, source_target_pairs={{0,4},{1,5},{2,6},{3,7},{12,8},{13,9},{14,10},{15,11},{16,20},{17,... | collective-permute-start | bytes 4423688 | tf_op jit(solution)/shard_map/ppermute | solution.py:249
  44.3 8.2 %collective-permute-done.22.refs_2_.refs_0_ = bf16[3840,128]{1,0:T(8,128)(2,1)} collective-permute-done((bf16[3840,128]{1,0:T(8,128)(2,1)}, bf16[3840,128]{1,0:T(8,128)(2,1)}, u32[]{:S(2)}, u32[]{:S(2)}) %collective-permute-start.22) | collective-permute-done | bytes 983072 | tf_op jit(solution)/shard_map/ppermute | solution.py:267
  66.4 19.3 %collective-permute-done.24.refs_0_ = bf16[192,3840]{1,0:T(8,128)(2,1)} collective-permute-done((bf16[192,3840]{1,0:T(8,128)(2,1)}, bf16[192,3840]{1,0:T(8,128)(2,1)}, u32[]{:S(2)}, u32[]{:S(2)}) %collective-permute-start.24) | collective-permute-done | bytes 1474592 | tf_op jit(solution)/shard_map/ppermute | solution.py:249
  87.2 28.7 %collective-permute-done.25.refs_1_ = bf16[192,3840]{1,0:T(8,128)(2,1)} collective-permute-done((bf16[192,3840]{1,0:T(8,128)(2,1)}, bf16[192,3840]{1,0:T(8,128)(2,1)}, u32[]{:S(2)}, u32[]{:S(2)}) %collective-permute-start.25) | collective-permute-done | bytes 1474592 | tf_op jit(solution)/shard_map/ppermute | solution.py:249
  119.8 5.5 %select_reduce_fusion = s32[384]{0:T(512)S(1)} fusion(s32[384]{0:T(512)S(1)} %iota_add_fusion, s32[12288]{0:T(1024)S(1)} %copy-done.20), kind=kLoop, calls=%fused_computation | loop fusion | flops 14155392 | bytes 52224 | tf_op jit(solution)/shard_map/reduce_sum | solution.py:341
  131.0 9.0 %collective-permute-done.10.refs_5_.refs_1_.refs_2_ = bf16[3840,128]{1,0:T(8,128)(2,1)} collective-permute-done((bf16[3840,128]{1,0:T(8,128)(2,1)S(1)}, bf16[3840,128]{1,0:T(8,128)(2,1)}, u32[]{:S(2)}, u32[]{:S(2)}) %collective-permute-start.10) | collective-permute-done | bytes 983072 | tf_op jit(solution)/shard_map/ppermute | solution.py:267
  159.5 5.6 %collective-permute-done.21.refs_3_.refs_0_ = bf16[3840,128]{1,0:T(8,128)(2,1)} collective-permute-done((bf16[3840,128]{1,0:T(8,128)(2,1)}, bf16[3840,128]{1,0:T(8,128)(2,1)}, u32[]{:S(2)}, u32[]{:S(2)}) %collective-permute-start.21) | collective-permute-done | bytes 983072 | tf_op jit(solution)/shard_map/ppermute | solution.py:267
  167.5 10.8 %collective-permute-done.11.refs_1_.refs_3_ = bf16[3840,128]{1,0:T(8,128)(2,1)} collective-permute-done((bf16[3840,128]{1,0:T(8,128)(2,1)}, bf16[3840,128]{1,0:T(8,128)(2,1)}, u32[]{:S(2)}, u32[]{:S(2)}) %collective-permute-start.11) | collective-permute-done | bytes 983072 | tf_op jit(solution)/shard_map/ppermute | solution.py:267
  178.3 28.6 %collective-permute-start.13 = (bf16[3840,128]{1,0:T(8,128)(2,1)}, bf16[3840,128]{1,0:T(8,128)(2,1)S(1)}, u32[]{:S(2)}, u32[]{:S(2)}) collective-permute-start(bf16[3840,128]{1,0:T(8,128)(2,1)} %copy-done.16), channel_id=1, source_target_pairs={{0,4},{1,5},{2,6},{3,7},{4,0},{5,1},{6,2},{7,3},{8,12},{9,13},{10,... | collective-permute-start | bytes 2949128 | tf_op jit(solution)/shard_map/ppermute | solution.py:267
  208.1 6.7 %shard_map.79.refs_5_ = f32[2,192,128]{2,1,0:T(8,128)S(1)} custom-call(s32[4]{0:T(128)S(1)} %get-tuple-element.56.spot_ref, bf16[192,61440]{1,0:T(8,128)(2,1)} %bitcast.81, bf16[3840,128]{1,0:T(8,128)(2,1)S(1)} %get-tuple-element.52.refs_0_.refs_1_.refs_2_.refs_3_, bf16[3840,128]{1,0:T(8,128)(2,1)S(1)} %get-tuple-element.51.refs_2_.refs_3_.refs_0_.refs_1_, ...), custom_call_target="tpu_custom_call" | custom-call | flops 754974720 | bytes 9830400 | tf_op jit(solution)/shard_map/pallas_call | solution.py:169
  224.6 5.0 %shard_map.80.refs_5_ = f32[2,192,128]{2,1,0:T(8,128)S(1)} custom-call(s32[4]{0:T(128)S(1)} %get-tuple-element.56.spot_ref, bf16[192,61440]{1,0:T(8,128)(2,1)} %bitcast.82, bf16[3840,128]{1,0:T(8,128)(2,1)} %collective-permute-done.7.refs_3_.refs_1_.refs_2_, bf16[3840,128]{1,0:T(8,128)(2,1)} %collective-permute-done.22.refs_2_.refs_0_, ...), custom_call_target="tpu_custom_call" | custom-call | flops 754974720 | bytes 9830400 | tf_op jit(solution)/shard_map/pallas_call | solution.py:169
  229.7 5.1 %shard_map.81.refs_5_ = f32[2,192,128]{2,1,0:T(8,128)S(1)} custom-call(s32[4]{0:T(128)S(1)} %get-tuple-element.56.spot_ref, bf16[192,61440]{1,0:T(8,128)(2,1)} %bitcast.83, bf16[3840,128]{1,0:T(8,128)(2,1)} %collective-permute-done.17.refs_1_, bf16[3840,128]{1,0:T(8,128)(2,1)} %collective-permute-done.10.refs_5_.refs_1_.refs_2_, ...), custom_call_target="tpu_custom_call" | custom-call | flops 754974720 | bytes 9830400 | tf_op jit(solution)/shard_map/pallas_call | solution.py:169
  234.7 4.7 %shard_map.82.refs_5_ = f32[2,192,128]{2,1,0:T(8,128)S(1)} custom-call(s32[4]{0:T(128)S(1)} %get-tuple-element.56.spot_ref, bf16[192,61440]{1,0:T(8,128)(2,1)} %bitcast.84, bf16[3840,128]{1,0:T(8,128)(2,1)} %collective-permute-done.14.refs_1_, bf16[3840,128]{1,0:T(8,128)(2,1)S(1)} %copy-done.5, bf16[3840,128]{1,0:T(8,128)(2,1)S(1)} %copy-done.8, ...), custom_call_target="tpu_custom_call" | custom-call | flops 754974720 | bytes 9830400 | tf_op jit(solution)/shard_map/pallas_call | solution.py:169
  241.4 5.0 %shard_map.83.refs_5_ = f32[2,192,128]{2,1,0:T(8,128)S(1)} custom-call(s32[4]{0:T(128)S(1)} %get-tuple-element.56.spot_ref, bf16[192,61440]{1,0:T(8,128)(2,1)} %bitcast.85, bf16[3840,128]{1,0:T(8,128)(2,1)} %collective-permute-done.16.refs_1_.refs_3_, bf16[3840,128]{1,0:T(8,128)(2,1)} %collective-permute-done.18.refs_2_, ...), custom_call_target="tpu_custom_call" | custom-call | flops 754974720 | bytes 9830400 | tf_op jit(solution)/shard_map/pallas_call | solution.py:169
  246.4 4.7 %shard_map.84.refs_5_ = f32[2,192,128]{2,1,0:T(8,128)S(1)} custom-call(s32[4]{0:T(128)S(1)} %get-tuple-element.56.spot_ref, bf16[192,61440]{1,0:T(8,128)(2,1)} %bitcast.86, bf16[3840,128]{1,0:T(8,128)(2,1)} %collective-permute-done.11.refs_1_.refs_3_, bf16[3840,128]{1,0:T(8,128)(2,1)} %collective-permute-done.12.refs_2_, ...), custom_call_target="tpu_custom_call" | custom-call | flops 754974720 | bytes 9830400 | tf_op jit(solution)/shard_map/pallas_call | solution.py:169
  251.2 11.5 %collective-permute-done.27.refs_0_.refs_2_.refs_3_ = bf16[3840,128]{1,0:T(8,128)(2,1)S(1)} collective-permute-done((bf16[3840,128]{1,0:T(8,128)(2,1)}, bf16[3840,128]{1,0:T(8,128)(2,1)S(1)}, u32[]{:S(2)}, u32[]{:S(2)}) %collective-permute-start.27) | collective-permute-done | bytes 983072 | tf_op jit(solution)/shard_map/ppermute | solution.py:267
  271.7 9.3 %collective-permute-start.32 = (bf16[3840,128]{1,0:T(8,128)(2,1)}, bf16[3840,128]{1,0:T(8,128)(2,1)}, u32[]{:S(2)}, u32[]{:S(2)}) collective-permute-start(bf16[3840,128]{1,0:T(8,128)(2,1)} %get-tuple-element.41), channel_id=1, source_target_pairs={{0,4},{1,5},{2,6},{3,7},{4,0},{5,1},{6,2},{7,3},{8,12},{9,13},{10,... | collective-permute-start | bytes 2949128 | tf_op jit(solution)/shard_map/ppermute | solution.py:267
  290.9 27.8 %all-to-all-done = f32[32,12,128]{2,1,0:T(8,128)S(1)} async-done(((f32[32,12,128]{2,1,0:T(8,128)}), f32[32,12,128]{2,1,0:T(8,128)S(1)}, u32[]{:S(2)}, u32[]{:S(2)}) %all-to-all-start) | async-done | bytes 196640 | tf_op jit(solution)/shard_map/all_to_all | solution.py:356
  329.7 5.0 %shard_map.91 = f32[2,192,128]{2,1,0:T(8,128)S(1)} custom-call(s32[4]{0:T(128)S(1)} %get-tuple-element.56.spot_ref, bf16[192,61440]{1,0:T(8,128)(2,1)} %bitcast.89, bf16[3840,128]{1,0:T(8,128)(2,1)} %collective-permute-done.30.refs_1_, bf16[3840,128]{1,0:T(8,128)(2,1)} %collective-permute-done.31.refs_2_, bf16[3840,128]{1,0:T(8,128)(2,1)} %collective-permute-done.32.refs_3_, ...), custom_call_target="tpu_custom_call" | custom-call | flops 754974720 | bytes 9830400 | tf_op jit(solution)/shard_map/pallas_call | solution.py:169
  335.8 6.1 %all-to-all-start.2 = ((f32[32,12,128]{2,1,0:T(8,128)}), f32[32,12,128]{2,1,0:T(8,128)S(1)}, u32[]{:S(2)}, u32[]{:S(2)}) async-start(f32[32,12,128]{2,1,0:T(8,128)} %reshape.229), calls=%async_computation.2 | async-start | bytes 524288 | tf_op jit(solution)/shard_map/all_to_all | solution.py:356
  343.4 9.7 %all-to-all-done.2 = f32[32,12,128]{2,1,0:T(8,128)S(1)} async-done(((f32[32,12,128]{2,1,0:T(8,128)}), f32[32,12,128]{2,1,0:T(8,128)S(1)}, u32[]{:S(2)}, u32[]{:S(2)}) %all-to-all-start.2) | async-done | bytes 196640 | tf_op jit(solution)/shard_map/all_to_all | solution.py:356
  357.2 9.6 %all-to-all-done.1 = f32[32,12,128]{2,1,0:T(8,128)S(1)} async-done(((f32[32,12,128]{2,1,0:T(8,128)}), f32[32,12,128]{2,1,0:T(8,128)S(1)}, u32[]{:S(2)}, u32[]{:S(2)}) %all-to-all-start.1) | async-done | bytes 196640 | tf_op jit(solution)/shard_map/all_to_all | solution.py:356
  370.0 10.6 %all-to-all-done.3 = f32[32,12,128]{2,1,0:T(8,128)S(1)} async-done(((f32[32,12,128]{2,1,0:T(8,128)}), f32[32,12,128]{2,1,0:T(8,128)S(1)}, u32[]{:S(2)}, u32[]{:S(2)}) %all-to-all-start.3) | async-done | bytes 196640 | tf_op jit(solution)/shard_map/all_to_all | solution.py:356
  (196 shorter events, 127.2 us)
Async XLA Ops:
  11.0 30.8 %collective-permute-start.4 = (bf16[3840,128]{1,0:T(8,128)(2,1)S(1)}, bf16[3840,128]{1,0:T(8,128)(2,1)}, u32[]{:S(2)}, u32[]{:S(2)}) collective-permute-start(bf16[3840,128]{1,0:T(8,128)(2,1)S(1)} %get-tuple-element.52.refs_0_.refs_1_.refs_2_.refs_3_), channel_id=1, source_target_pairs={{4,8},{5,9},{6,10},{7,11},{8,4},{9,5},{10,6},{11,7},{20,24},{21,25... | collective-permute-start | bytes 2949128 | tf_op jit(solution)/shard_map/ppermute | solution.py:267
  16.2 36.4 %collective-permute-start.22 = (bf16[3840,128]{1,0:T(8,128)(2,1)}, bf16[3840,128]{1,0:T(8,128)(2,1)}, u32[]{:S(2)}, u32[]{:S(2)}) collective-permute-start(bf16[3840,128]{1,0:T(8,128)(2,1)} %get-tuple-element.36), channel_id=1, source_target_pairs={{0,2},{1,3},{2,0},{3,1},{4,6},{5,7},{6,4},{7,5},{8,10},{9,11},{10,... | collective-permute-start | bytes 2949128 | tf_op jit(solution)/shard_map/ppermute | solution.py:267
  37.0 48.7 %collective-permute-start.24 = (bf16[192,3840]{1,0:T(8,128)(2,1)}, bf16[192,3840]{1,0:T(8,128)(2,1)}, u32[]{:S(2)}, u32[]{:S(2)}) collective-permute-start(bf16[192,3840]{1,0:T(8,128)(2,1)} %get-tuple-element.50), channel_id=1, source_target_pairs={{0,4},{1,5},{2,6},{3,7},{12,8},{13,9},{14,10},{15,11},{16,20},{17,... | collective-permute-start | bytes 4423688 | tf_op jit(solution)/shard_map/ppermute | solution.py:249
  41.8 74.0 %collective-permute-start.25 = (bf16[192,3840]{1,0:T(8,128)(2,1)}, bf16[192,3840]{1,0:T(8,128)(2,1)}, u32[]{:S(2)}, u32[]{:S(2)}) collective-permute-start(bf16[192,3840]{1,0:T(8,128)(2,1)} %get-tuple-element.49), channel_id=1, source_target_pairs={{0,4},{1,5},{2,6},{3,7},{12,8},{13,9},{14,10},{15,11},{16,20},{17,... | collective-permute-start | bytes 4423688 | tf_op jit(solution)/shard_map/ppermute | solution.py:249
  54.5 63.0 %collective-permute-start.20 = (bf16[3840,128]{1,0:T(8,128)(2,1)}, bf16[3840,128]{1,0:T(8,128)(2,1)}, u32[]{:S(2)}, u32[]{:S(2)}) collective-permute-start(bf16[3840,128]{1,0:T(8,128)(2,1)} %collective-permute-done.19.refs_4_.refs_3_), channel_id=1, source_target_pairs={{4,8},{5,9},{6,10},{7,11},{8,4},{9,5},{10,6},{11,7},{20,24},{21,25... | collective-permute-start | bytes 2949128 | tf_op jit(solution)/shard_map/ppermute | solution.py:267
  56.1 62.4 %collective-permute-start.5 = (bf16[3840,128]{1,0:T(8,128)(2,1)}, bf16[3840,128]{1,0:T(8,128)(2,1)}, u32[]{:S(2)}, u32[]{:S(2)}) collective-permute-start(bf16[3840,128]{1,0:T(8,128)(2,1)} %collective-permute-done.4.refs_2_.refs_6_), channel_id=1, source_target_pairs={{4,0},{5,1},{6,2},{7,3},{8,12},{9,13},{10,14},{11,15},{20,16},{21,... | collective-permute-start | bytes 2949128 | tf_op jit(solution)/shard_map/ppermute | solution.py:267
  61.8 63.5 %collective-permute-start.14 = (bf16[3840,128]{1,0:T(8,128)(2,1)}, bf16[3840,128]{1,0:T(8,128)(2,1)}, u32[]{:S(2)}, u32[]{:S(2)}) collective-permute-start(bf16[3840,128]{1,0:T(8,128)(2,1)} %get-tuple-element.33), channel_id=1, source_target_pairs={{0,1},{1,0},{2,3},{3,2},{4,5},{5,4},{6,7},{7,6},{8,9},{9,8},{10,11... | collective-permute-start | bytes 2949128 | tf_op jit(solution)/shard_map/ppermute | solution.py:267
  85.7 41.2 %collective-permute-start.8 = (bf16[3840,128]{1,0:T(8,128)(2,1)}, bf16[3840,128]{1,0:T(8,128)(2,1)S(1)}, u32[]{:S(2)}, u32[]{:S(2)}) collective-permute-start(bf16[3840,128]{1,0:T(8,128)(2,1)} %copy-done.17), channel_id=1, source_target_pairs={{0,2},{1,3},{2,0},{3,1},{4,6},{5,7},{6,4},{7,5},{8,10},{9,11},{10,... | collective-permute-start | bytes 2949128 | tf_op jit(solution)/shard_map/ppermute | solution.py:267
  158.1 61.9 %collective-permute-start.28 = (bf16[3840,128]{1,0:T(8,128)(2,1)}, bf16[3840,128]{1,0:T(8,128)(2,1)S(1)}, u32[]{:S(2)}, u32[]{:S(2)}) collective-permute-start(bf16[3840,128]{1,0:T(8,128)(2,1)} %collective-permute-done.9.refs_3_.refs_4_), channel_id=1, source_target_pairs={{4,0},{5,1},{6,2},{7,3},{8,12},{9,13},{10,14},{11,15},{20,16},{21,... | collective-permute-start | bytes 2949128 | tf_op jit(solution)/shard_map/ppermute | solution.py:267
  159.4 61.3 %collective-permute-start.16 = (bf16[3840,128]{1,0:T(8,128)(2,1)}, bf16[3840,128]{1,0:T(8,128)(2,1)}, u32[]{:S(2)}, u32[]{:S(2)}) collective-permute-start(bf16[3840,128]{1,0:T(8,128)(2,1)} %shard_map.78), channel_id=1, source_target_pairs={{0,1},{1,0},{2,3},{3,2},{4,5},{5,4},{6,7},{7,6},{8,9},{9,8},{10,11... | collective-permute-start | bytes 2949128 | tf_op jit(solution)/shard_map/ppermute | solution.py:267
  165.1 57.7 %collective-permute-start.12 = (bf16[3840,128]{1,0:T(8,128)(2,1)}, bf16[3840,128]{1,0:T(8,128)(2,1)}, u32[]{:S(2)}, u32[]{:S(2)}) collective-permute-start(bf16[3840,128]{1,0:T(8,128)(2,1)} %get-tuple-element.31), channel_id=1, source_target_pairs={{0,2},{1,3},{2,0},{3,1},{4,6},{5,7},{6,4},{7,5},{8,10},{9,11},{10,... | collective-permute-start | bytes 2949128 | tf_op jit(solution)/shard_map/ppermute | solution.py:267
  166.6 55.8 %collective-permute-start.18 = (bf16[3840,128]{1,0:T(8,128)(2,1)}, bf16[3840,128]{1,0:T(8,128)(2,1)}, u32[]{:S(2)}, u32[]{:S(2)}) collective-permute-start(bf16[3840,128]{1,0:T(8,128)(2,1)} %collective-permute-done.17.refs_1_), channel_id=1, source_target_pairs={{0,2},{1,3},{2,0},{3,1},{4,6},{5,7},{6,4},{7,5},{8,10},{9,11},{10,... | collective-permute-start | bytes 2949128 | tf_op jit(solution)/shard_map/ppermute | solution.py:267
  178.3 61.8 %collective-permute-start.13 = (bf16[3840,128]{1,0:T(8,128)(2,1)}, bf16[3840,128]{1,0:T(8,128)(2,1)S(1)}, u32[]{:S(2)}, u32[]{:S(2)}) collective-permute-start(bf16[3840,128]{1,0:T(8,128)(2,1)} %copy-done.16), channel_id=1, source_target_pairs={{0,4},{1,5},{2,6},{3,7},{4,0},{5,1},{6,2},{7,3},{8,12},{9,13},{10,... | collective-permute-start | bytes 2949128 | tf_op jit(solution)/shard_map/ppermute | solution.py:267
  220.0 48.1 %collective-permute-start.36 = (bf16[3840,128]{1,0:T(8,128)(2,1)S(1)}, bf16[3840,128]{1,0:T(8,128)(2,1)S(1)}, u32[]{:S(2)}, u32[]{:S(2)}) collective-permute-start(bf16[3840,128]{1,0:T(8,128)(2,1)S(1)} %get-tuple-element.51.refs_2_.refs_3_.refs_0_.refs_1_), channel_id=1, source_target_pairs={{4,8},{5,9},{6,10},{7,11},{8,4},{9,5},{10,6},{11,7},{20,24},{21,25... | collective-permute-start | bytes 2949128 | tf_op jit(solution)/shard_map/ppermute | solution.py:267
  220.7 49.3 %collective-permute-start.34 = (bf16[3840,128]{1,0:T(8,128)(2,1)S(1)}, bf16[3840,128]{1,0:T(8,128)(2,1)S(1)}, u32[]{:S(2)}, u32[]{:S(2)}) collective-permute-start(bf16[3840,128]{1,0:T(8,128)(2,1)S(1)} %shard_map.88), channel_id=1, source_target_pairs={{0,2},{1,3},{2,0},{3,1},{4,6},{5,7},{6,4},{7,5},{8,10},{9,11},{10,... | collective-permute-start | bytes 2949128 | tf_op jit(solution)/shard_map/ppermute | solution.py:267
  222.4 40.3 %collective-permute-start.27 = (bf16[3840,128]{1,0:T(8,128)(2,1)}, bf16[3840,128]{1,0:T(8,128)(2,1)S(1)}, u32[]{:S(2)}, u32[]{:S(2)}) collective-permute-start(bf16[3840,128]{1,0:T(8,128)(2,1)} %get-tuple-element.38), channel_id=1, source_target_pairs={{0,2},{1,3},{2,0},{3,1},{4,6},{5,7},{6,4},{7,5},{8,10},{9,11},{10,... | collective-permute-start | bytes 2949128 | tf_op jit(solution)/shard_map/ppermute | solution.py:267
  222.8 58.2 %collective-permute-start.37 = (bf16[3840,128]{1,0:T(8,128)(2,1)S(1)}, bf16[3840,128]{1,0:T(8,128)(2,1)S(1)}, u32[]{:S(2)}, u32[]{:S(2)}) collective-permute-start(bf16[3840,128]{1,0:T(8,128)(2,1)S(1)} %get-tuple-element.42), channel_id=1, source_target_pairs={{0,1},{1,0},{2,3},{3,2},{4,5},{5,4},{6,7},{7,6},{8,9},{9,8},{10,11... | collective-permute-start | bytes 2949128 | tf_op jit(solution)/shard_map/ppermute | solution.py:267
  240.1 31.6 %collective-permute-start.26 = (f32[192,128]{1,0:T(8,128)S(1)}, f32[192,128]{1,0:T(8,128)S(1)}, u32[]{:S(2)}, u32[]{:S(2)}) collective-permute-start(f32[192,128]{1,0:T(8,128)S(1)} %slice_bitcast_fusion.2), channel_id=1, source_target_pairs={{4,0},{5,1},{6,2},{7,3},{8,12},{9,13},{10,14},{11,15},{20,16},{21,... | collective-permute-start | bytes 294920 | tf_op jit(solution)/shard_map/ppermute | solution.py:290
  262.7 62.3 %collective-permute-start.35 = (bf16[3840,128]{1,0:T(8,128)(2,1)}, bf16[3840,128]{1,0:T(8,128)(2,1)}, u32[]{:S(2)}, u32[]{:S(2)}) collective-permute-start(bf16[3840,128]{1,0:T(8,128)(2,1)} %collective-permute-done.11.refs_1_.refs_3_), channel_id=1, source_target_pairs={{4,0},{5,1},{6,2},{7,3},{8,12},{9,13},{10,14},{11,15},{20,16},{21,... | collective-permute-start | bytes 2949128 | tf_op jit(solution)/shard_map/ppermute | solution.py:267
  269.0 60.6 %collective-permute-start.30 = (bf16[3840,128]{1,0:T(8,128)(2,1)}, bf16[3840,128]{1,0:T(8,128)(2,1)}, u32[]{:S(2)}, u32[]{:S(2)}) collective-permute-start(bf16[3840,128]{1,0:T(8,128)(2,1)} %get-tuple-element.39), channel_id=1, source_target_pairs={{0,1},{1,0},{2,3},{3,2},{4,5},{5,4},{6,7},{7,6},{8,9},{9,8},{10,11... | collective-permute-start | bytes 2949128 | tf_op jit(solution)/shard_map/ppermute | solution.py:267
  271.0 58.6 %collective-permute-start.31 = (bf16[3840,128]{1,0:T(8,128)(2,1)}, bf16[3840,128]{1,0:T(8,128)(2,1)}, u32[]{:S(2)}, u32[]{:S(2)}) collective-permute-start(bf16[3840,128]{1,0:T(8,128)(2,1)} %get-tuple-element.40), channel_id=1, source_target_pairs={{0,2},{1,3},{2,0},{3,1},{4,6},{5,7},{6,4},{7,5},{8,10},{9,11},{10,... | collective-permute-start | bytes 2949128 | tf_op jit(solution)/shard_map/ppermute | solution.py:267
  271.7 57.9 %collective-permute-start.32 = (bf16[3840,128]{1,0:T(8,128)(2,1)}, bf16[3840,128]{1,0:T(8,128)(2,1)}, u32[]{:S(2)}, u32[]{:S(2)}) collective-permute-start(bf16[3840,128]{1,0:T(8,128)(2,1)} %get-tuple-element.41), channel_id=1, source_target_pairs={{0,4},{1,5},{2,6},{3,7},{4,0},{5,1},{6,2},{7,3},{8,12},{9,13},{10,... | collective-permute-start | bytes 2949128 | tf_op jit(solution)/shard_map/ppermute | solution.py:267
  282.0 47.7 %collective-permute-start.33 = (bf16[3840,128]{1,0:T(8,128)(2,1)S(1)}, bf16[3840,128]{1,0:T(8,128)(2,1)}, u32[]{:S(2)}, u32[]{:S(2)}) collective-permute-start(bf16[3840,128]{1,0:T(8,128)(2,1)S(1)} %collective-permute-done.27.refs_0_.refs_2_.refs_3_), channel_id=1, source_target_pairs={{4,8},{5,9},{6,10},{7,11},{8,4},{9,5},{10,6},{11,7},{20,24},{21,25... | collective-permute-start | bytes 2949128 | tf_op jit(solution)/shard_map/ppermute | solution.py:267
  284.8 33.9 %all-to-all-start = ((f32[32,12,128]{2,1,0:T(8,128)}), f32[32,12,128]{2,1,0:T(8,128)S(1)}, u32[]{:S(2)}, u32[]{:S(2)}) async-start(f32[32,12,128]{2,1,0:T(8,128)} %reshape.222), calls=%async_computation | async-start | bytes 524288 | tf_op jit(solution)/shard_map/all_to_all | solution.py:356
  (44 other events, 1128.6 us)
